TPU v7x, 32 devices: a whole 2x2x4 slice. The times are simulated.
32 devices in a mesh: batch: 8 (over z, y), fsdp: 4 (over x, core).
Axes of the slice: x: 2, y: 2, z: 4, core: 2. Of those that a mesh axis runs over, the one named last changes fastest.
Arguments:
- tokens: bfloat16 [128, 256, 768], P(('batch', 'fsdp')), may hold values from -6 to 6
- cotangent: bfloat16 [128, 256, 768], P(('batch', 'fsdp')), may hold values from -6 to 6
- mask_pos: int32 [128, 128], P(('batch', 'fsdp')), may hold values from 0 to 255, as said below
- mask_count: int32 [128], P(('batch', 'fsdp')), may hold values from 8 to 128, as said below
- w_qkv: float32 [768, 2304], P('fsdp'), may hold values from -0.21875 to 0.21875
- m_qkv: float32 [768, 2304], P(('fsdp', 'batch')), may hold values from -217.2232 to 217.2232
- v_qkv: float32 [768, 2304], P(('fsdp', 'batch')), may hold values from 1474.56 to 23592.96
- w_out: float32 [768, 768], P('fsdp'), may hold values from -0.875 to 0.875
- m_out: float32 [768, 768], P(('fsdp', 'batch')), may hold values from -50.685413 to 50.685413
- v_out: float32 [768, 768], P(('fsdp', 'batch')), may hold values from 80.2816 to 1284.5056
- w_fc1: float32 [768, 3072], P('fsdp'), may hold values from -0.21875 to 0.21875
- m_fc1: float32 [768, 3072], P(('fsdp', 'batch')), may hold values from -86.88928 to 86.88928
- v_fc1: float32 [768, 3072], P(('fsdp', 'batch')), may hold values from 235.9296 to 3774.8735
- w_fc2: float32 [3072, 768], P('fsdp'), may hold values from -0.109375 to 0.109375
- m_fc2: float32 [3072, 768], P(('fsdp', 'batch')), may hold values from -181.01933 to 181.01933
- v_fc2: float32 [3072, 768], P(('fsdp', 'batch')), may hold values from 1024 to 16384
- vectors: float32 [14, 768], P(None, 'fsdp'), may hold values from -1.2 to 1.6
- m_vec: float32 [14, 768], P(None, ('fsdp', 'batch')), may hold values from -217.2232 to 217.2232
- v_vec: float32 [14, 768], P(None, ('fsdp', 'batch')), may hold values from 1474.56 to 23592.96
Outputs:
- layer_out: bfloat16 [128, 256, 768], P(('batch', 'fsdp'))
- grad_tokens: float32 [128, 256, 768], P(('batch', 'fsdp'))
- new_w_qkv: float32 [768, 2304], P('fsdp')
- new_m_qkv: float32 [768, 2304], P(('fsdp', 'batch'))
- new_v_qkv: float32 [768, 2304], P(('fsdp', 'batch'))
- new_w_out: float32 [768, 768], P('fsdp')
- new_m_out: float32 [768, 768], P(('fsdp', 'batch'))
- new_v_out: float32 [768, 768], P(('fsdp', 'batch'))
- new_w_fc1: float32 [768, 3072], P('fsdp')
- new_m_fc1: float32 [768, 3072], P(('fsdp', 'batch'))
- new_v_fc1: float32 [768, 3072], P(('fsdp', 'batch'))
- new_w_fc2: float32 [3072, 768], P('fsdp')
- new_m_fc2: float32 [3072, 768], P(('fsdp', 'batch'))
- new_v_fc2: float32 [3072, 768], P(('fsdp', 'batch'))
- new_vectors: float32 [14, 768], P(None, 'fsdp')
- new_m_vec: float32 [14, 768], P(None, ('fsdp', 'batch'))
- new_v_vec: float32 [14, 768], P(None, ('fsdp', 'batch'))
Inputs may be any that keep to these rules, and one draw needn't show every extreme that they name: `mask_pos`: each row holds 128 different positions of the pair; its first mask_count entries are the masked tokens. `mask_count`: some pair has 128 masked tokens.
All inputs are finite; a program needn't handle non-finite values.
Results may differ from a plain program's by a relative error of at most 0.015.
Values may be sent and summed in bfloat16 or wider, within the bound.
No kernel may reach another device: no remote copies, remote signals or barrier semaphores. Data moves between devices by JAX's collectives and lax.ppermute only.
A program may use at most 192 MiB of HBM per device.

v0:
```python
import math
import jax
import jax.numpy as jnp
from jax import lax
from jax.sharding import PartitionSpec as P

D = 768
HEADS = 12
HDIM = 64
FF = 3072
TEXT = 40
STEP = 3
MAXM = 128
BETA_ONE = 0.5
BETA_TWO = 0.5
EPS_ADAM = 1e-08
STEP_RATES = (0.03, 0.1, 0.03, 0.015, 0.3)
DECAY_RATES = (0.01, 0.01, 0.01, 0.01, 0.0)
INV_ROOT_TWO = 1.0 / math.sqrt(2.0)
INV_ROOT_TWOPI = 1.0 / math.sqrt(2.0 * math.pi)


def dot_first(left_mat, right_mat):
    return lax.dot_general(
        left_mat, right_mat, (((0,), (0,)), ((), ())), preferred_element_type=jnp.float32
    )


def dot_last(left_mat, right_mat):
    return lax.dot_general(
        left_mat, right_mat, (((1,), (1,)), ((), ())), preferred_element_type=jnp.float32
    )


def normalize(hidden):
    row_mean = jnp.mean(hidden, axis=-1, keepdims=True)
    centred = hidden - row_mean
    inv_scale = lax.rsqrt(jnp.mean(centred * centred, axis=-1, keepdims=True) + 1e-06)
    return (centred * inv_scale, inv_scale)


def norm_back(gradient, normed, inv_scale, gain_row):
    scaled = gradient * gain_row
    return inv_scale * (
        scaled
        - jnp.mean(scaled, axis=-1, keepdims=True)
        - normed * jnp.mean(scaled * normed, axis=-1, keepdims=True)
    )


def adamw(weight, gradient, moment_one, moment_two, step_rate, decay_rate):
    new_first = BETA_ONE * moment_one + (1.0 - BETA_ONE) * gradient
    new_second = BETA_TWO * moment_two + (1.0 - BETA_TWO) * gradient * gradient
    correct_one = 1.0 - BETA_ONE**STEP
    correct_two = 1.0 - BETA_TWO**STEP
    update = (
        new_first / correct_one / (jnp.sqrt(new_second / correct_two) + EPS_ADAM)
        + decay_rate * weight
    )
    return (weight - step_rate * update, new_first, new_second)


def shards(
    tokens,
    cotangent,
    mask_pos,
    mask_count,
    w_qkv,
    m_qkv,
    v_qkv,
    w_out,
    m_out,
    v_out,
    w_fc1,
    m_fc1,
    v_fc1,
    w_fc2,
    m_fc2,
    v_fc2,
    vectors,
    m_vec,
    v_vec,
):
    pair_count, length, model_width = tokens.shape
    token_rows = pair_count * length
    fc1_parts = FF // D
    attn_scale = HDIM ** (-0.5)
    shard_qkv = w_qkv.astype(jnp.bfloat16)
    shard_out = w_out.astype(jnp.bfloat16)
    shard_fc1 = w_fc1.astype(jnp.bfloat16)
    shard_fc2 = w_fc2.astype(jnp.bfloat16)
    shard_vec = vectors.astype(jnp.bfloat16)
    qkv_w, out_w, fc1_w, fc2_w, vec_low = (
        lax.all_gather(shard_qkv, "fsdp", axis=0, tiled=True),
        lax.all_gather(shard_out, "fsdp", axis=0, tiled=True),
        lax.all_gather(shard_fc1, "fsdp", axis=0, tiled=True),
        lax.all_gather(shard_fc2, "fsdp", axis=0, tiled=True),
        lax.all_gather(shard_vec, "fsdp", axis=1, tiled=True),
    )
    vector_rows = vec_low.astype(jnp.float32)
    is_image = lax.broadcasted_iota(jnp.int32, (length, 1), 0) >= TEXT
    stream_zero = tokens.astype(jnp.float32) + jnp.where(is_image, vector_rows[1], vector_rows[0])
    stream_zero = stream_zero.reshape(token_rows, model_width)
    normed_one, scale_one = normalize(stream_zero)
    input_one = (normed_one * vector_rows[2] + vector_rows[3]).astype(jnp.bfloat16)
    qkv_bias = jnp.concatenate(
        [vector_rows[4], jnp.zeros((model_width,), jnp.float32), vector_rows[5]]
    )
    qkv_all = (jnp.dot(input_one, qkv_w, preferred_element_type=jnp.float32) + qkv_bias).astype(
        jnp.bfloat16
    )
    head_view = qkv_all.reshape(pair_count, length, 3, HEADS, HDIM)
    queries = head_view[:, :, 0]
    keys_all = head_view[:, :, 1]
    values_all = head_view[:, :, 2]
    scores = (
        jnp.einsum("pqhe,pkhe->pqhk", queries, keys_all, preferred_element_type=jnp.float32)
        * attn_scale
    )
    row_max = jnp.max(scores, axis=-1, keepdims=True)
    log_total = row_max + jnp.log(jnp.sum(jnp.exp(scores - row_max), axis=-1, keepdims=True))
    attn_low = jnp.exp(scores - log_total).astype(jnp.bfloat16)
    mixed_heads = jnp.einsum(
        "pqhk,pkhe->pqhe", attn_low, values_all, preferred_element_type=jnp.float32
    )
    mixed_heads = mixed_heads.astype(jnp.bfloat16).reshape(token_rows, model_width)
    stream_one = (
        stream_zero
        + jnp.dot(mixed_heads, out_w, preferred_element_type=jnp.float32)
        + vector_rows[6]
    )
    normed_two, scale_two = normalize(stream_one)
    input_two = (normed_two * vector_rows[7] + vector_rows[8]).astype(jnp.bfloat16)
    preact = jnp.dot(input_two, fc1_w, preferred_element_type=jnp.float32) + vector_rows[
        9 : 9 + fc1_parts
    ].reshape(FF)
    activated = jax.nn.gelu(preact, approximate=False).astype(jnp.bfloat16)
    result = (
        stream_one
        + jnp.dot(activated, fc2_w, preferred_element_type=jnp.float32)
        + vector_rows[9 + fc1_parts]
    )
    layer_out = result.astype(jnp.bfloat16).reshape(pair_count, length, model_width)
    qkv_w, out_w, fc1_w, fc2_w, vec_low = (
        lax.all_gather(shard_qkv, "fsdp", axis=0, tiled=True),
        lax.all_gather(shard_out, "fsdp", axis=0, tiled=True),
        lax.all_gather(shard_fc1, "fsdp", axis=0, tiled=True),
        lax.all_gather(shard_fc2, "fsdp", axis=0, tiled=True),
        lax.all_gather(shard_vec, "fsdp", axis=1, tiled=True),
    )
    vector_rows = vec_low.astype(jnp.float32)
    slot_index = lax.broadcasted_iota(jnp.int32, (pair_count, MAXM), 1)
    slot_live = slot_index < mask_count[:, None]
    positions = lax.broadcasted_iota(jnp.int32, (pair_count, MAXM, length), 2)
    keep_rows = jnp.any((mask_pos[:, :, None] == positions) & slot_live[:, :, None], axis=1)
    chosen = keep_rows.shape[1]
    picked = pair_count * chosen

    def select(values):
        shaped = values.reshape((pair_count, length) + values.shape[1:])
        return shaped.reshape((picked,) + values.shape[1:])

    def spread_back(values):
        shaped = values.reshape((pair_count, chosen) + values.shape[1:])
        return shaped.reshape((token_rows,) + values.shape[1:])

    grad_out = select(
        cotangent.reshape(token_rows, model_width).astype(jnp.float32)
    ) * keep_rows.reshape(picked, 1).astype(jnp.float32)
    grad_low = grad_out.astype(jnp.bfloat16)
    grad_fc2 = dot_first(select(activated), grad_low)
    bias_fc2 = jnp.sum(grad_out, axis=0)
    grad_act = dot_last(grad_low, fc2_w)
    preact_sel = select(preact)
    gelu_slope = (
        0.5 * (1.0 + lax.erf(preact_sel * INV_ROOT_TWO))
        + preact_sel * jnp.exp(-0.5 * preact_sel * preact_sel) * INV_ROOT_TWOPI
    )
    grad_pre = grad_act * gelu_slope
    bias_fc1 = jnp.sum(grad_pre, axis=0)
    pre_low = grad_pre.astype(jnp.bfloat16)
    grad_fc1 = dot_first(select(input_two), pre_low)
    grad_norm_two = dot_last(pre_low, fc1_w)
    normed_two_sel = select(normed_two)
    gain_two = jnp.sum(grad_norm_two * normed_two_sel, axis=0)
    shift_two = jnp.sum(grad_norm_two, axis=0)
    grad_stream = grad_out + norm_back(
        grad_norm_two, normed_two_sel, select(scale_two), vector_rows[7]
    )
    bias_out = jnp.sum(grad_stream, axis=0)
    stream_low = grad_stream.astype(jnp.bfloat16)
    grad_outw = dot_first(select(mixed_heads), stream_low)
    grad_mixed = (
        dot_last(stream_low, out_w).astype(jnp.bfloat16).reshape(pair_count, chosen, HEADS, HDIM)
    )
    queries_sel = select(queries.reshape(token_rows, HEADS, HDIM)).reshape(
        pair_count, chosen, HEADS, HDIM
    )
    total_sel = select(log_total.reshape(token_rows, HEADS, 1)).reshape(
        pair_count, chosen, HEADS, 1
    )
    scores_again = (
        jnp.einsum("pqhe,pkhe->pqhk", queries_sel, keys_all, preferred_element_type=jnp.float32)
        * attn_scale
    )
    attn_again = jnp.exp(scores_again - total_sel)
    grad_values = jnp.einsum(
        "pqhk,pqhe->pkhe",
        attn_again.astype(jnp.bfloat16),
        grad_mixed,
        preferred_element_type=jnp.float32,
    )
    grad_attn = jnp.einsum(
        "pqhe,pkhe->pqhk", grad_mixed, values_all, preferred_element_type=jnp.float32
    )
    grad_scores = attn_again * (grad_attn - jnp.sum(attn_again * grad_attn, axis=-1, keepdims=True))
    grad_scores = grad_scores.astype(jnp.bfloat16)
    grad_queries = (
        jnp.einsum("pqhk,pkhe->pqhe", grad_scores, keys_all, preferred_element_type=jnp.float32)
        * attn_scale
    )
    grad_keys = (
        jnp.einsum("pqhk,pqhe->pkhe", grad_scores, queries_sel, preferred_element_type=jnp.float32)
        * attn_scale
    )
    grad_queries = spread_back(grad_queries.reshape(picked, model_width))
    grad_values = grad_values.reshape(token_rows, model_width)
    grad_qkv = jnp.concatenate(
        [grad_queries, grad_keys.reshape(token_rows, model_width), grad_values], axis=1
    )
    bias_query = jnp.sum(grad_queries, axis=0)
    bias_value = jnp.sum(grad_values, axis=0)
    qkv_low = grad_qkv.astype(jnp.bfloat16)
    grad_qkvw = dot_first(input_one, qkv_low)
    grad_norm_one = dot_last(qkv_low, qkv_w)
    gain_one = jnp.sum(grad_norm_one * normed_one, axis=0)
    shift_one = jnp.sum(grad_norm_one, axis=0)
    grad_input = spread_back(grad_stream) + norm_back(
        grad_norm_one, normed_one, scale_one, vector_rows[2]
    )
    grad_shaped = grad_input.reshape(pair_count, length, model_width)
    type_text = jnp.sum(jnp.where(is_image, 0.0, grad_shaped), axis=(0, 1))
    type_image = jnp.sum(jnp.where(is_image, grad_shaped, 0.0), axis=(0, 1))
    grad_vec = jnp.concatenate(
        [
            jnp.stack(
                [
                    type_text,
                    type_image,
                    gain_one,
                    shift_one,
                    bias_query,
                    bias_value,
                    bias_out,
                    gain_two,
                    shift_two,
                ]
            ),
            bias_fc1.reshape(fc1_parts, model_width),
            bias_fc2[None, :],
        ],
        axis=0,
    )
    halfway = (
        lax.psum_scatter(
            grad_qkvw.astype(jnp.bfloat16), "fsdp", scatter_dimension=0, tiled=True
        ).astype(jnp.float32),
        lax.psum_scatter(
            grad_outw.astype(jnp.bfloat16), "fsdp", scatter_dimension=0, tiled=True
        ).astype(jnp.float32),
        lax.psum_scatter(
            grad_fc1.astype(jnp.bfloat16), "fsdp", scatter_dimension=0, tiled=True
        ).astype(jnp.float32),
        lax.psum_scatter(
            grad_fc2.astype(jnp.bfloat16), "fsdp", scatter_dimension=0, tiled=True
        ).astype(jnp.float32),
        lax.psum_scatter(
            grad_vec.astype(jnp.bfloat16), "fsdp", scatter_dimension=1, tiled=True
        ).astype(jnp.float32),
    )
    owned = (
        lax.psum_scatter(halfway[0], "batch", scatter_dimension=0, tiled=True),
        lax.psum_scatter(halfway[1], "batch", scatter_dimension=0, tiled=True),
        lax.psum_scatter(halfway[2], "batch", scatter_dimension=0, tiled=True),
        lax.psum_scatter(halfway[3], "batch", scatter_dimension=0, tiled=True),
        lax.psum_scatter(halfway[4], "batch", scatter_dimension=1, tiled=True),
    )
    batch_index = lax.axis_index("batch")
    masters = (w_qkv, w_out, w_fc1, w_fc2, vectors)
    firsts = (m_qkv, m_out, m_fc1, m_fc2, m_vec)
    seconds = (v_qkv, v_out, v_fc1, v_fc2, v_vec)
    alongs = (0, 0, 0, 0, 1)
    updated = []
    for master, gradient, moment_one, moment_two, along, step_rate, decay_rate in zip(
        masters, owned, firsts, seconds, alongs, STEP_RATES, DECAY_RATES
    ):
        slice_rows = gradient.shape[along]
        own_slice = lax.dynamic_slice_in_dim(master, batch_index * slice_rows, slice_rows, along)
        updated.append(adamw(own_slice, gradient, moment_one, moment_two, step_rate, decay_rate))
    new_masters = (
        lax.all_gather(updated[0][0].astype(jnp.bfloat16), "batch", axis=0, tiled=True).astype(
            jnp.float32
        ),
        lax.all_gather(updated[1][0].astype(jnp.bfloat16), "batch", axis=0, tiled=True).astype(
            jnp.float32
        ),
        lax.all_gather(updated[2][0].astype(jnp.bfloat16), "batch", axis=0, tiled=True).astype(
            jnp.float32
        ),
        lax.all_gather(updated[3][0].astype(jnp.bfloat16), "batch", axis=0, tiled=True).astype(
            jnp.float32
        ),
        lax.all_gather(updated[4][0].astype(jnp.bfloat16), "batch", axis=1, tiled=True).astype(
            jnp.float32
        ),
    )
    return (
        layer_out,
        grad_shaped,
        new_masters[0],
        updated[0][1],
        updated[0][2],
        new_masters[1],
        updated[1][1],
        updated[1][2],
        new_masters[2],
        updated[2][1],
        updated[2][2],
        new_masters[3],
        updated[3][1],
        updated[3][2],
        new_masters[4],
        updated[4][1],
        updated[4][2],
    )


def solution(mesh):
    placed = (
        P(("batch", "fsdp"), None, None),
        P(("batch", "fsdp"), None, None),
        P(("batch", "fsdp"), None),
        P(("batch", "fsdp")),
        P("fsdp", None),
        P(("fsdp", "batch"), None),
        P(("fsdp", "batch"), None),
        P("fsdp", None),
        P(("fsdp", "batch"), None),
        P(("fsdp", "batch"), None),
        P("fsdp", None),
        P(("fsdp", "batch"), None),
        P(("fsdp", "batch"), None),
        P("fsdp", None),
        P(("fsdp", "batch"), None),
        P(("fsdp", "batch"), None),
        P(None, "fsdp"),
        P(None, ("fsdp", "batch")),
        P(None, ("fsdp", "batch")),
    )
    return jax.shard_map(
        shards,
        mesh=mesh,
        in_specs=placed,
        out_specs=(
            P(("batch", "fsdp"), None, None),
            P(("batch", "fsdp"), None, None),
            P("fsdp", None),
            P(("fsdp", "batch"), None),
            P(("fsdp", "batch"), None),
            P("fsdp", None),
            P(("fsdp", "batch"), None),
            P(("fsdp", "batch"), None),
            P("fsdp", None),
            P(("fsdp", "batch"), None),
            P(("fsdp", "batch"), None),
            P("fsdp", None),
            P(("fsdp", "batch"), None),
            P(("fsdp", "batch"), None),
            P(None, "fsdp"),
            P(None, ("fsdp", "batch")),
            P(None, ("fsdp", "batch")),
        ),
        check_vma=False,
    )
```

profile of v0, /device:TPU:0, one launch (start us, length us, event | category | flops | bytes accessed | tf_op | source)
XLA Modules:
  0.0 737.7 jit_solution(3257606192598027593)
XLA Ops:
  7.3 2.6 convert_element_type.148
  12.1 2.9 convert_element_type.157
  15.1 6.2 all-gather
  23.6 2.2 multiply_reduce_fusion.6
  29.4 14.3 %all-gather.9.cloned.1.call-done = bf16[768,2304]{1,0:T(8,128)(2,1)} async-done(((bf16[192,2304]{1,0:T(8,128)(2,1)}), bf16[768,2304]{1,0:T(8,128)(2,1)}) %all-gather.9.cloned.1.call-update) | async-done | bytes 3538960 | tf_op jit(solution)/shard_map/all_gather | solution.py:94
  43.6 8.4 %add_convert_fusion = bf16[1024,2304]{1,0:T(8,128)(2,1)} fusion(bf16[1024,768]{1,0:T(8,128)(2,1)} %add_convert_fusion.3, bf16[768,2304]{1,0:T(8,128)(2,1)} %all-gather.9.cloned.1.call-done, f32[2304]{0:T(1024)S(1)} %pad_maximum_fusion), kind=kOutput, calls=%fused_computation.36 | convolution fusion | flops 3628597248 | bytes 9839616 | tf_op jit(solution)/shard_map/dot_general | solution.py:109
  52.1 6.8 copy.97
  58.9 8.9 %reshape.233 = bf16[4,256,3,12,64]{1,0,4,3,2:T(4,128)(2,1)} reshape(bf16[1024,2304]{0,1:T(8,128)(2,1)} %copy.97) | data formatting | bytes 9437184 | tf_op jit(solution)/shard_map/reshape | solution.py:112
  67.8 3.3 fusion.59
  73.0 2.7 fusion.12
  77.8 2.4 fusion.28
  82.9 3.5 fusion.61
  88.6 14.3 %all-gather.13.cloned.1.call-done = bf16[768,3072]{1,0:T(8,128)(2,1)} async-done(((bf16[192,3072]{1,0:T(8,128)(2,1)}), bf16[768,3072]{1,0:T(8,128)(2,1)}) %all-gather.13.cloned.1.call-update) | async-done | bytes 4718608 | tf_op jit(solution)/shard_map/all_gather | solution.py:96
  102.9 37.7 %fusion.2 = (bf16[1024,3072]{1,0:T(8,128)(2,1)}, f32[1024,3072]{1,0:T(8,128)}) fusion(f32[3072]{0:T(1024)S(1)} %add.230, bf16[768,3072]{1,0:T(8,128)(2,1)} %all-gather.13.cloned.1.call-done, f32[1024,768]{1,0:T(8,128)} %copy-done.12, f32[768]{0:T(1024)S(1)} %get-tuple-element.28, f32[768]{0:T(1024)S(1)} %get-tuple-element.29, f32[1024]{0:T(1024)S(1)} %add_rsqrt_fusion, ...), kind=kOutput, calls=%fused_computation.4 | convolution fusion | flops 5043388416 | bytes 26765312 | tf_op jit(solution)/shard_map/dot_general | solution.py:134
  141.7 11.9 %fusion.62 = (bf16[3072]{0:T(1024)(128)(2,1)S(1)}, bf16[1024,3072]{1,0:T(8,128)(2,1)S(1)}) fusion(f32[1024,3072]{1,0:T(8,128)} %get-tuple-element.69, f32[3072]{0:T(1024)S(1)} %add.230, bf16[1024,768]{1,0:T(8,128)(2,1)S(1)} %copy-done.23, bf16[3072,768]{1,0:T(8,128)(2,1)} %all-gather.15.cloned.1.call-done), kind=kOutput, calls=%fused_computation.151 | convolution fusion | flops 4869583872 | bytes 25184256 | tf_op jit(solution)/shard_map/dot_general | solution.py:30
  153.6 2.6 copy-done.51
  156.3 7.8 %convolution_convert_fusion.1 = bf16[768,3072]{1,0:T(8,128)(2,1)} fusion(bf16[1024,3072]{1,0:T(8,128)(2,1)S(1)} %get-tuple-element.79, f32[1024,768]{1,0:T(8,128)S(1)} %copy-done.13, f32[768]{0:T(1024)S(1)} %get-tuple-element.28, f32[768]{0:T(1024)S(1)} %get-tuple-element.29, f32[1024]{0:T(1024)S(1)} %add_rsqrt_fusion, f32[1024]{0:T(1024)S(1)} %broadcast_multiply_fusion.4), kind=kOutput, calls=%fused_computation.39 | convolution fusion | flops 4838129664 | bytes 14170112 | tf_op jit(solution)/shard_map/dot_general | solution.py:24
  164.2 9.7 %convolution_convert_fusion = bf16[3072,768]{1,0:T(8,128)(2,1)} fusion(bf16[1024,3072]{1,0:T(8,128)(2,1)} %get-tuple-element.68, bf16[1024,768]{1,0:T(8,128)(2,1)S(1)} %copy-done.23), kind=kOutput, calls=%fused_computation.38 | convolution fusion | flops 4834197504 | bytes 12582912 | tf_op jit(solution)/shard_map/dot_general | solution.py:24
  174.0 10.4 %multiply_reduce_fusion.1 = (bf16[768]{0:T(1024)(128)(2,1)S(1)}, f32[1024]{0:T(1024)S(1)}, f32[1024]{0:T(1024)S(1)}, bf16[768]{0:T(1024)(128)(2,1)S(1)}, f32[1024,768]{1,0:T(8,128)S(1)}) fusion(f32[1024,768]{1,0:T(8,128)} %copy-done.12, f32[1024]{0:T(1024)S(1)} %add_rsqrt_fusion, f32[1024]{0:T(1024)S(1)} %broadcast_multiply_fusion.4, ...), kind=kOutput, calls=%fused_computation.51 | convolution fusion | flops 4838912000 | bytes 17324032 | tf_op jit(solution)/shard_map/dot_general | solution.py:30
  191.0 8.7 %bitcast_convert_fusion = (bf16[4,256,12,64]{1,3,2,0:T(8,128)(2,1)S(1)}, f32[4,12,64,256]{3,2,1,0:T(8,128)}) fusion(f32[4,12,256,256]{3,2,1,0:T(8,128)} %copy-done, f32[4,256,12]{1,2,0:T(8,128)S(1)} %log_add_fusion, bf16[4,256,12,64]{1,0,3,2:T(4,128)(2,1)S(1)} %reshape.236), kind=kOutput, calls=%fused_computation.42 | convolution fusion | flops 412876800 | bytes 18923520 | tf_op jit(solution)/shard_map/pqhk,pqhe->pkhe/dot_general | solution.py:207
  202.4 2.4 convolution_convert_fusion.5
  204.9 9.0 %fusion.8 = (f32[4,256,12]{1,2,0:T(8,128)S(1)}, f32[4,12,256,256]{3,2,1,0:T(8,128)}) fusion(f32[4,12,256,256]{3,2,1,0:T(8,128)} %copy-done, f32[4,256,12]{1,2,0:T(8,128)S(1)} %log_add_fusion, bf16[4,256,12,64]{1,0,3,2:T(4,128)(2,1)S(1)} %reshape.236, bf16[4,256,1,12,64]{1,0,4,3,2:T(4,128)(2,1)S(1)} %copy-done.4), kind=kOutput, calls=%fused_computation.12 | convolution fusion | flops 415223808 | bytes 28409856 | tf_op jit(solution)/shard_map/pqhe,pkhe->pqhk/dot_general | solution.py:213
  214.0 11.4 %fusion.10 = bf16[4,256,12,256]{1,3,2,0:T(8,128)(2,1)S(1)} fusion(f32[4,12,256,256]{3,2,1,0:T(8,128)} %get-tuple-element.72, f32[4,12,256,256]{3,2,1,0:T(8,128)} %copy-done, f32[4,256,12]{1,2,0:T(8,128)S(1)} %get-tuple-element.71, f32[4,256,12]{1,2,0:T(8,128)S(1)} %log_add_fusion), kind=kLoop, calls=%fused_computation.14 | loop fusion | flops 15728640 | bytes 31555584 | tf_op jit(solution)/shard_map/convert_element_type | solution.py:217
  225.4 2.6 bitcast_convert_fusion.1
  237.3 5.5 convolution_convert_fusion.2
  242.8 3.0 convert_element_type.177
  245.9 16.8 %reduce-scatter.25.cloned.1.call-done = bf16[768,768]{1,0:T(8,128)(2,1)} async-done(((bf16[3072,768]{1,0:T(8,128)(2,1)}), bf16[768,768]{1,0:T(8,128)(2,1)}) %reduce-scatter.25.cloned.1.call-update) | async-done | bytes 1179664 | tf_op jit(solution)/shard_map/reduce_scatter | solution.py:274
  262.6 2.8 convert_element_type.181
  266.1 2.3 bitcast_reduce_fusion.1
  270.8 8.8 %multiply_reduce_fusion.2 = (bf16[768]{0:T(1024)(128)(2,1)S(1)}, f32[1024]{0:T(1024)S(1)}, f32[1024]{0:T(1024)S(1)}, bf16[768]{0:T(1024)(128)(2,1)S(1)}, f32[1024,768]{1,0:T(8,128)S(1)}) fusion(f32[4,256,768]{2,1,0:T(8,128)S(1)} %copy-done.2, f32[1024]{0:T(1024)S(1)} %bitcast.176, f32[1024]{0:T(1024)S(1)} %bitcast.173, f32[768]{0:T(1024)S(1)} %copy-done.32, ...), kind=kOutput, calls=%fused_computation.52 | convolution fusion | flops 3630952960 | bytes 14571520 | tf_op jit(solution)/shard_map/dot_general | solution.py:30
  279.6 3.1 select_reduce_fusion
  283.7 7.7 %reduce-scatter.17.cloned.1.call-done = bf16[192,768]{1,0:T(8,128)(2,1)} async-done(((bf16[768,768]{1,0:T(8,128)(2,1)}), bf16[192,768]{1,0:T(8,128)(2,1)}) %reduce-scatter.17.cloned.1.call-update) | async-done | bytes 294928 | tf_op jit(solution)/shard_map/reduce_scatter | solution.py:268
  293.3 41.0 %reduce-scatter.13.cloned.1.call-done = bf16[192,2304]{1,0:T(8,128)(2,1)} async-done(((bf16[768,2304]{1,0:T(8,128)(2,1)}), bf16[192,2304]{1,0:T(8,128)(2,1)}) %reduce-scatter.13.cloned.1.call-update) | async-done | bytes 884752 | tf_op jit(solution)/shard_map/reduce_scatter | solution.py:265
  334.4 2.5 convert_element_type.169
  337.0 71.3 %reduce-scatter.23.cloned.1.call-done = f32[24,3072]{1,0:T(8,128)} async-done(((f32[192,3072]{1,0:T(8,128)}), f32[24,3072]{1,0:T(8,128)}) %reduce-scatter.23.cloned.1.call-update) | async-done | bytes 294928 | tf_op jit(solution)/shard_map/reduce_scatter | solution.py:284
  411.7 69.4 %reduce-scatter.27.cloned.1.call-done = f32[96,768]{1,0:T(8,128)} async-done(((f32[768,768]{1,0:T(8,128)}), f32[96,768]{1,0:T(8,128)}) %reduce-scatter.27.cloned.1.call-update) | async-done | bytes 294928 | tf_op jit(solution)/shard_map/reduce_scatter | solution.py:285
  481.1 2.2 subtract_convert_fusion
  483.5 9.5 %add_convert_fusion.1 = bf16[1024,768]{1,0:T(8,128)(2,1)} fusion(f32[1024,768]{1,0:T(8,128)S(1)} %copy-done.15, bf16[1024,3072]{1,0:T(8,128)(2,1)} %get-tuple-element.68, bf16[3072,768]{1,0:T(8,128)(2,1)} %all-gather.15.cloned.1.call-done, f32[768]{0:T(1024)S(1)} %copy-done.44), kind=kOutput, calls=%fused_computation.63 | convolution fusion | flops 4834197504 | bytes 15731712 | tf_op jit(solution)/shard_map/dot_general | solution.py:140
  492.9 10.2 %reduce-scatter.29.cloned.1.call-done = bf16[192,14]{1,0:T(8,128)(2,1)} async-done(((bf16[768,14]{1,0:T(8,128)(2,1)}), bf16[192,14]{1,0:T(8,128)(2,1)}) %reduce-scatter.29.cloned.1.call-update) | async-done | bytes 5392
  504.0 37.2 %all-reduce = f32[14,192]{1,0:T(8,128)S(1)} all-reduce(bf16[14,192]{1,0:T(8,128)(2,1)S(1)} %copy.118), channel_id=11, replica_groups=mesh['batch'=8,'fsdp'=4] {'batch'}, use_global_device_ids=true, to_apply=%region_32.33.clone | all-reduce | flops 2688 | bytes 16128
  541.9 30.7 %all-gather.1 = bf16[8,24,14]{1,2,0:T(8,128)(2,1)S(1)} all-gather(bf16[1,24,14]{1,2,0:T(8,128)(2,1)S(1)} %get-tuple-element.37), channel_id=1, replica_groups=mesh['batch'=8,'fsdp'=4] {'batch'}, dimensions={0}, use_global_device_ids=true | all-gather | bytes 6048 | tf_op jit(solution)/shard_map/all_gather | solution.py:313
  574.9 31.4 %all_gather.41 = bf16[192,768]{1,0:T(8,128)(2,1)S(1)} all-gather(bf16[24,768]{1,0:T(8,128)(2,1)S(1)} %get-tuple-element.49), channel_id=1, replica_groups=mesh['batch'=8,'fsdp'=4] {'batch'}, dimensions={0}, use_global_device_ids=true | all-gather | bytes 331776 | tf_op jit(solution)/shard_map/all_gather | solution.py:304
  607.2 32.5 %reduce-scatter.15.cloned.1.call-done = f32[24,2304]{1,0:T(8,128)} async-done(((f32[192,2304]{1,0:T(8,128)}), f32[24,2304]{1,0:T(8,128)}) %reduce-scatter.15.cloned.1.call-update) | async-done | bytes 221200 | tf_op jit(solution)/shard_map/reduce_scatter | solution.py:282
  641.7 33.8 %all_gather.40 = bf16[192,2304]{1,0:T(8,128)(2,1)S(1)} all-gather(bf16[24,2304]{1,0:T(8,128)(2,1)S(1)} %get-tuple-element.52), channel_id=1, replica_groups=mesh['batch'=8,'fsdp'=4] {'batch'}, dimensions={0}, use_global_device_ids=true | all-gather | bytes 995328 | tf_op jit(solution)/shard_map/all_gather | solution.py:301
  676.8 8.8 %all-gather.17.cloned.1.call-done = bf16[192,3072]{1,0:T(8,128)(2,1)} async-done(((bf16[24,3072]{1,0:T(8,128)(2,1)}), bf16[192,3072]{1,0:T(8,128)(2,1)}) %all-gather.17.cloned.1.call-update) | async-done | bytes 1179664 | tf_op jit(solution)/shard_map/all_gather | solution.py:307
  685.6 2.9 convert_element_type.179
  688.6 39.3 %all-gather.19.cloned.1.call-done = bf16[768,768]{1,0:T(8,128)(2,1)} async-done(((bf16[96,768]{1,0:T(8,128)(2,1)}), bf16[768,768]{1,0:T(8,128)(2,1)}) %all-gather.19.cloned.1.call-update) | async-done | bytes 1179664 | tf_op jit(solution)/shard_map/all_gather | solution.py:310
  727.9 2.8 convert_element_type.183
  (212 shorter events, 53.4 us)
Async XLA Ops:
  7.2 36.4 %all-gather.9.cloned.1.call-start = ((), (), s32[]{:S(2)}) async-start(), calls=%async_computation.9 | async-start | bytes 4423680 | tf_op jit(solution)/shard_map/all_gather | solution.py:94
  9.9 73.0 %all-gather.11.cloned.1.call-start = ((), (), s32[]{:S(2)}) async-start(), calls=%async_computation.10 | async-start | bytes 1474560 | tf_op jit(solution)/shard_map/all_gather | solution.py:95
  10.7 92.1 %all-gather.13.cloned.1.call-start = ((), (), s32[]{:S(2)}) async-start(), calls=%async_computation.11 | async-start | bytes 5898240 | tf_op jit(solution)/shard_map/all_gather | solution.py:96
  12.0 10.1 %copy-start.49 = (s32[4]{0:T(128)S(1)}, s32[4]{0:T(128)}, u32[]{:S(2)}) copy-start(s32[4]{0:T(128)} %param.22) | copy-start | bytes 52
  12.0 10.2 %copy-start.45 = (s32[4,128]{1,0:T(4,128)S(1)}, s32[4,128]{1,0:T(4,128)}, u32[]{:S(2)}) copy-start(s32[4,128]{1,0:T(4,128)} %param.21) | copy-start | bytes 6148
  12.0 11.1 %copy-start.20 = (bf16[4,256,768]{2,1,0:T(8,128)(2,1)S(1)}, bf16[4,256,768]{2,1,0:T(8,128)(2,1)}, u32[]{:S(2)}) copy-start(bf16[4,256,768]{2,1,0:T(8,128)(2,1)} %param.19) | copy-start | bytes 4718596
  12.0 129.7 %all-gather.15.cloned.1.call-start = ((), (), s32[]{:S(2)}) async-start(), calls=%async_computation.12 | async-start | bytes 5898240 | tf_op jit(solution)/shard_map/all_gather | solution.py:97
  15.0 227.8 %reduce-scatter.21.cloned.1.call-start = ((), (), s32[]{:S(2)}) async-start(), calls=%async_computation.17 | async-start | bytes 5898240 | tf_op jit(solution)/shard_map/reduce_scatter | solution.py:271
  15.1 8.0 %copy-start.46 = (pred[256]{0:T(512)(128)(4,1)}, pred[256]{0:T(512)(128)(4,1)S(1)}, u32[]{:S(2)}) copy-start(pred[256]{0:T(512)(128)(4,1)S(1)} %iota_compare_fusion.2) | copy-start | bytes 772
  22.1 5.6 copy-start.31
  23.6 4.0 copy-start.33
  25.8 57.1 %copy-start.1 = (f32[4,256,768]{2,1,0:T(8,128)}, f32[4,256,768]{2,1,0:T(8,128)S(1)}, u32[]{:S(2)}) copy-start(f32[4,256,768]{2,1,0:T(8,128)S(1)} %get-tuple-element.59) | copy-start | bytes 9437188
  71.1 4.6 copy-start.3
  73.0 4.8 copy-start
  102.9 38.9 %copy-start.23 = (bf16[1024,768]{1,0:T(8,128)(2,1)S(1)}, bf16[1024,768]{1,0:T(8,128)(2,1)}, u32[]{:S(2)}) copy-start(bf16[1024,768]{1,0:T(8,128)(2,1)} %fusion.27) | copy-start | bytes 4718596
  141.7 14.5 %copy-start.13 = (f32[1024,768]{1,0:T(8,128)S(1)}, f32[1024,768]{1,0:T(8,128)}, u32[]{:S(2)}) copy-start(f32[1024,768]{1,0:T(8,128)} %copy-done.12) | copy-start | bytes 9437188
  164.1 98.5 %reduce-scatter.25.cloned.1.call-start = ((), (), s32[]{:S(2)}) async-start(), calls=%async_computation.20 | async-start | bytes 5898240 | tf_op jit(solution)/shard_map/reduce_scatter | solution.py:274
  173.9 10.5 %copy-start.8 = (bf16[4,256,768]{2,1,0:T(8,128)(2,1)S(1)}, bf16[4,256,768]{2,1,0:T(8,128)(2,1)}, u32[]{:S(2)}) copy-start(bf16[4,256,768]{2,1,0:T(8,128)(2,1)} %param.20) | copy-start | bytes 4718596
  174.0 10.5 %copy-start.38 = (f32[1,2,4,128]{3,1,2,0:T(2,128)S(1)}, f32[1,2,4,128]{3,1,2,0:T(2,128)}, u32[]{:S(2)}) copy-start(f32[1,2,4,128]{3,1,2,0:T(2,128)} %copy-done.37) | copy-start | bytes 12292
  174.0 117.5 %reduce-scatter.17.cloned.1.call-start = ((), (), s32[]{:S(2)}) async-start(), calls=%async_computation.15 | async-start | bytes 1474560 | tf_op jit(solution)/shard_map/reduce_scatter | solution.py:268
  174.0 10.4 %copy-start.14 = (f32[1024,768]{1,0:T(8,128)S(1)}, f32[1024,768]{1,0:T(8,128)}, u32[]{:S(2)}) copy-start(f32[1024,768]{1,0:T(8,128)} %copy-done.12) | copy-start | bytes 9437188
  213.9 120.5 %reduce-scatter.13.cloned.1.call-start = ((), (), s32[]{:S(2)}) async-start(), calls=%async_computation.13 | async-start | bytes 4423680 | tf_op jit(solution)/shard_map/reduce_scatter | solution.py:265
  214.0 11.4 %copy-start.11 = (bf16[4,256,1,12,64]{1,0,4,3,2:T(4,128)(2,1)S(1)}, bf16[4,256,1,12,64]{1,0,4,3,2:T(4,128)(2,1)}, u32[]{:S(2)}) copy-start(bf16[4,256,1,12,64]{1,0,4,3,2:T(4,128)(2,1)} %copy-done.10) | copy-start | bytes 4718596
  242.7 165.5 %reduce-scatter.23.cloned.1.call-start = ((), (), s32[]{:S(2)}) async-start(), calls=%async_computation.18 | async-start | bytes 2654208 | tf_op jit(solution)/shard_map/reduce_scatter | solution.py:284
  245.8 19.8 %copy-start.47 = (pred[256]{0:T(512)(128)(4,1)S(1)}, pred[256]{0:T(512)(128)(4,1)}, u32[]{:S(2)}) copy-start(pred[256]{0:T(512)(128)(4,1)} %copy-done.46) | copy-start | bytes 772
  245.8 19.8 %copy-start.9 = (bf16[4,256,768]{2,1,0:T(8,128)(2,1)S(1)}, bf16[4,256,768]{2,1,0:T(8,128)(2,1)}, u32[]{:S(2)}) copy-start(bf16[4,256,768]{2,1,0:T(8,128)(2,1)} %param.20) | copy-start | bytes 4718596
  245.8 19.8 %copy-start.41 = (f32[4,256]{1,0:T(4,128)S(1)}, f32[4,256]{1,0:T(4,128)}, u32[]{:S(2)}) copy-start(f32[4,256]{1,0:T(4,128)} %get-tuple-element.62) | copy-start | bytes 12292
  245.8 235.3 %reduce-scatter.27.cloned.1.call-start = ((), (), s32[]{:S(2)}) async-start(), calls=%async_computation.21 | async-start | bytes 2654208 | tf_op jit(solution)/shard_map/reduce_scatter | solution.py:285
  265.5 237.6 %reduce-scatter.29.cloned.1.call-start = ((), (), s32[]{:S(2)}) async-start(), calls=%async_computation.23 | async-start | bytes 245760
  266.1 4.7 copy-start.2
  266.1 4.7 copy-start.32
  266.1 4.6 copy-start.34
  266.1 4.6 copy-start.36
  270.8 8.8 %copy-start.18 = (f32[1024,768]{1,0:T(8,128)S(1)}, f32[1024,768]{1,0:T(8,128)}, u32[]{:S(2)}) copy-start(f32[1024,768]{1,0:T(8,128)} %copy-done.16) | copy-start | bytes 9437188
  282.8 125.5 %copy-start.27 = (f32[24,3072]{1,0:T(8,128)S(1)}, f32[24,3072]{1,0:T(8,128)}, u32[]{:S(2)}) copy-start(f32[24,3072]{1,0:T(8,128)} %param.30) | copy-start | bytes 884740
  283.7 289.6 %reduce-scatter.19.cloned.1.call-start = ((), (), s32[]{:S(2)}) async-start(), calls=%async_computation.16 | async-start | bytes 663552 | tf_op jit(solution)/shard_map/reduce_scatter | solution.py:283
  293.3 117.2 %copy-start.50 = (u32[32]{0:T(128)S(1)}, u32[32]{0:T(128)}, u32[]{:S(2)}) copy-start(u32[32]{0:T(128)} %constant.159) | copy-start | bytes 388
  293.3 346.4 %reduce-scatter.15.cloned.1.call-start = ((), (), s32[]{:S(2)}) async-start(), calls=%async_computation.14 | async-start | bytes 1990656 | tf_op jit(solution)/shard_map/reduce_scatter | solution.py:282
  336.9 146.5 %copy-start.15 = (f32[1024,768]{1,0:T(8,128)S(1)}, f32[1024,768]{1,0:T(8,128)}, u32[]{:S(2)}) copy-start(f32[1024,768]{1,0:T(8,128)} %copy-done.12) | copy-start | bytes 9437188
  336.9 146.5 %copy-start.44 = (f32[768]{0:T(1024)S(1)}, f32[768]{0:T(1024)}, u32[]{:S(2)}) copy-start(f32[768]{0:T(1024)} %get-tuple-element.27) | copy-start | bytes 9220
  336.9 348.7 %all-gather.17.cloned.1.call-start = ((), (), s32[]{:S(2)}) async-start(), calls=%async_computation.19 | async-start | bytes 1327104 | tf_op jit(solution)/shard_map/all_gather | solution.py:307
  410.4 317.4 %all-gather.19.cloned.1.call-start = ((), (), s32[]{:S(2)}) async-start(), calls=%async_computation.22 | async-start | bytes 1327104 | tf_op jit(solution)/shard_map/all_gather | solution.py:310
  483.4 57.8 %copy-start.40 = (f32[14,192]{1,0:T(8,128)S(1)}, f32[14,192]{1,0:T(8,128)}, u32[]{:S(2)}) copy-start(f32[14,192]{1,0:T(8,128)} %param.35) | copy-start | bytes 32260
  483.4 57.8 %copy-start.42 = (f32[14,24]{1,0:T(8,128)S(1)}, f32[14,24]{1,0:T(8,128)}, u32[]{:S(2)}) copy-start(f32[14,24]{1,0:T(8,128)} %param.36) | copy-start | bytes 4036
  483.4 57.8 %copy-start.43 = (f32[14,24]{1,0:T(8,128)S(1)}, f32[14,24]{1,0:T(8,128)}, u32[]{:S(2)}) copy-start(f32[14,24]{1,0:T(8,128)} %param.37) | copy-start | bytes 4036
  483.4 89.9 %copy-start.29 = (f32[24,768]{1,0:T(8,128)S(1)}, f32[24,768]{1,0:T(8,128)}, u32[]{:S(2)}) copy-start(f32[24,768]{1,0:T(8,128)} %param.27) | copy-start | bytes 221188
  483.4 89.9 %copy-start.30 = (f32[24,768]{1,0:T(8,128)S(1)}, f32[24,768]{1,0:T(8,128)}, u32[]{:S(2)}) copy-start(f32[24,768]{1,0:T(8,128)} %param.28) | copy-start | bytes 221188
  483.5 156.2 %copy-start.28 = (f32[24,2304]{1,0:T(8,128)S(1)}, f32[24,2304]{1,0:T(8,128)}, u32[]{:S(2)}) copy-start(f32[24,2304]{1,0:T(8,128)} %param.24) | copy-start | bytes 663556
  (19 other events, 46.6 us)
Sparse Core Ops, SparseCore 0:
  10.2 33.4 all-gather.8
  45.8 17.4 all-gather.10
  65.4 37.4 all-gather.12
  104.3 37.4 all-gather.14
  164.2 47.9 reduce-scatter.20
  214.6 47.9 reduce-scatter.24
  265.8 25.6 reduce-scatter.16
  294.0 40.3 reduce-scatter.12
  338.5 69.7 reduce-scatter.22
  412.2 68.8 reduce-scatter.26
  484.2 18.9 reduce-scatter.28
  506.9 62.8 reduce-scatter.18
  573.8 65.7 reduce-scatter.14
  642.3 43.3 all-gather.16
  687.7 40.1 all-gather.18
where the time goes:
time: 744 us; the launch traced here: 738 us
  waiting for transfers between devices  327 us (44%)
  matrix products  144 us (19%)
  blocking collectives  139 us (19%)
  other arithmetic  65.4 us (9%)
  local copies, waits for them, and re-layouts  45.8 us (6%)
  between operations  16 us (2%)
    reduce_scatter x1, waiting for transfers between devices, shards(): lax.psum_scatter(halfway[2], 'batch', scatter_dimension=0, tiled=True)  71.3 us
    reduce_scatter x1, waiting for transfers between devices, shards(): lax.psum_scatter(halfway[3], 'batch', scatter_dimension=0, tiled=True)  69.4 us
    reduce_scatter x1, waiting for transfers between devices, shards(): lax.psum_scatter(grad_qkvw.astype(jnp.bfloat16), 'fsdp', scatter_dimensio...  41 us
    all_gather x1, waiting for transfers between devices, shards(): lax.all_gather(updated[3][0].astype(jnp.bfloat16), 'batch', axis=0, tiled...  39.3 us
    dot_general x1, matrix products, shards(): jnp.dot(input_two, fc1_w, preferred_element_type=jnp.float32)  37.7 us
    unnamed x1, blocking collectives  37.2 us
    all_gather x1, blocking collectives, shards(): lax.all_gather(updated[0][0].astype(jnp.bfloat16), 'batch', axis=0, tiled...  33.8 us
    reduce_scatter x1, waiting for transfers between devices, shards(): lax.psum_scatter(halfway[0], 'batch', scatter_dimension=0, tiled=True)  32.5 us
  transfers between devices with their start and end apart: 15, of which 12 were waited for; matrix products, arithmetic and copies ran while one was open for 30% of the time, Pallas kernels for 0%

commit v1 on v0

--- a/solution.py
+++ b/solution.py
@@ -18,6 +18,27 @@
 DECAY_RATES = (0.01, 0.01, 0.01, 0.01, 0.0)
 INV_ROOT_TWO = 1.0 / math.sqrt(2.0)
 INV_ROOT_TWOPI = 1.0 / math.sqrt(2.0 * math.pi)
+
+
+def note_region_here(u, axis_k):
+    d_next = list(u.shape[1:])
+    d_next[axis_k] *= u.shape[0]
+    return jnp.moveaxis(u, 0, axis_k).reshape(d_next)
+
+
+def follow_series_all_by_axis(incoming_x, axis_key):
+    block_last = incoming_x[None]
+    p_count = lax.axis_size(axis_key)
+    for idx in range(p_count.bit_length() - 1):
+        long_array = 1 << idx
+        grid = []
+        for dd in tuple(range(p_count)):
+            grid.append((dd, dd ^ long_array))
+        before = lax.ppermute(block_last, axis_key, grid)
+        after = jnp.stack([block_last, before])
+        side_arr = lax.axis_index(axis_key) >> idx & 1
+        block_last = jnp.where(side_arr == 0, after, after[::-1]).reshape(-1, *incoming_x.shape)
+    return block_last
 
 
 def dot_first(left_mat, right_mat):
@@ -297,6 +318,10 @@
         slice_rows = gradient.shape[along]
         own_slice = lax.dynamic_slice_in_dim(master, batch_index * slice_rows, slice_rows, along)
         updated.append(adamw(own_slice, gradient, moment_one, moment_two, step_rate, decay_rate))
+
+    def plan_the_shifts_all(patch, arr_in, in_dim):
+        return note_region_here(follow_series_all_by_axis(patch, arr_in), in_dim)
+
     new_masters = (
         lax.all_gather(updated[0][0].astype(jnp.bfloat16), "batch", axis=0, tiled=True).astype(
             jnp.float32
@@ -307,9 +332,7 @@
         lax.all_gather(updated[2][0].astype(jnp.bfloat16), "batch", axis=0, tiled=True).astype(
             jnp.float32
         ),
-        lax.all_gather(updated[3][0].astype(jnp.bfloat16), "batch", axis=0, tiled=True).astype(
-            jnp.float32
-        ),
+        plan_the_shifts_all(updated[3][0].astype(jnp.bfloat16), "batch", 0).astype(jnp.float32),
         lax.all_gather(updated[4][0].astype(jnp.bfloat16), "batch", axis=1, tiled=True).astype(
             jnp.float32
         ),

time: 744 us -> 696 us (0.935)
  waiting for transfers between devices: 327 us -> 275 us
    reduce_scatter x1, waiting for transfers between devices: 69.4 us -> 3.43 us  [shards(): lax.psum_scatter(halfway[3], 'batch', scatter_dimension=0, tiled=True)]
    reduce_scatter x1, waiting for transfers between devices: 0.01 us -> 63.1 us  [shards(): lax.psum_scatter(halfway[1], 'batch', scatter_dimension=0, tiled=True)]
    reduce_scatter x1, waiting for transfers between devices: 32.5 us -> 73.6 us  [shards(): lax.psum_scatter(halfway[0], 'batch', scatter_dimension=0, tiled=True)]
    all_gather x1 -> x0, waiting for transfers between devices: 39.3 us -> none  [shards(): lax.all_gather(updated[3][0].astype(jnp.bfloat16), 'batch', axis=0, tiled...]
    reduce_scatter x1, waiting for transfers between devices: 71.3 us -> 40.5 us  [shards(): lax.psum_scatter(halfway[2], 'batch', scatter_dimension=0, tiled=True)]
    reduce_scatter x1, waiting for transfers between devices: 16.8 us -> 0.02 us  [shards(): lax.psum_scatter(grad_fc2.astype(jnp.bfloat16), 'fsdp', scatter_dimension...]
    reduce_scatter x1, waiting for transfers between devices: 0.02 us -> 9.7 us  [shards(): lax.psum_scatter(grad_fc1.astype(jnp.bfloat16), 'fsdp', scatter_dimension...]
    reduce_scatter x1, waiting for transfers between devices: 7.7 us -> 0.02 us  [shards(): lax.psum_scatter(grad_outw.astype(jnp.bfloat16), 'fsdp', scatter_dimensio...]
  transfers between devices with their start and end apart: 15 -> 17, of which waited for: 12 -> 10; matrix products, arithmetic and copies ran while one was open for 30% -> 35% of each run, Pallas kernels for 0% -> 0%
where the time goes in v1:
time: 696 us; the launch traced here: 690 us
  waiting for transfers between devices  275 us (40%)
  matrix products  147 us (21%)
  blocking collectives  141 us (20%)
  other arithmetic  61.2 us (9%)
  local copies, waits for them, and re-layouts  47.6 us (7%)
  between operations  16 us (2%)
    reduce_scatter x1, waiting for transfers between devices, shards(): lax.psum_scatter(halfway[0], 'batch', scatter_dimension=0, tiled=True)  73.6 us
    reduce_scatter x1, waiting for transfers between devices, shards(): lax.psum_scatter(halfway[1], 'batch', scatter_dimension=0, tiled=True)  63.1 us
    reduce_scatter x1, waiting for transfers between devices, shards(): lax.psum_scatter(halfway[2], 'batch', scatter_dimension=0, tiled=True)  40.5 us
    reduce_scatter x1, waiting for transfers between devices, shards(): lax.psum_scatter(grad_qkvw.astype(jnp.bfloat16), 'fsdp', scatter_dimensio...  38.4 us
    unnamed x1, blocking collectives  37.7 us
    dot_general x1, matrix products, shards(): jnp.dot(input_two, fc1_w, preferred_element_type=jnp.float32)  36.9 us
    dot_general x4, matrix products, dot_last(): lax.dot_general(left_mat, right_mat, (((1,), (1,)), ((), ())), preferred_...  34.7 us
    all_gather x1, blocking collectives, shards(): lax.all_gather(updated[0][0].astype(jnp.bfloat16), 'batch', axis=0, tiled...  34.1 us
  transfers between devices with their start and end apart: 17, of which 10 were waited for; matrix products, arithmetic and copies ran while one was open for 35% of the time, Pallas kernels for 0%

profile of v1, /device:TPU:0, one launch (start us, length us, event | category | flops | bytes accessed | tf_op | source)
XLA Modules:
  0.0 690.5 jit_solution(1789816122157430045)
XLA Ops:
  7.3 2.6 convert_element_type.151
  12.1 2.9 convert_element_type.160
  15.1 6.2 all-gather
  29.4 14.2 %all-gather.8.cloned.1.call-done = bf16[768,2304]{1,0:T(8,128)(2,1)} async-done(((bf16[192,2304]{1,0:T(8,128)(2,1)}), bf16[768,2304]{1,0:T(8,128)(2,1)}) %all-gather.8.cloned.1.call-update) | async-done | bytes 3538960 | tf_op jit(solution)/shard_map/all_gather | solution.py:115
  43.6 8.4 %add_convert_fusion = bf16[1024,2304]{1,0:T(8,128)(2,1)} fusion(bf16[1024,768]{1,0:T(8,128)(2,1)} %add_convert_fusion.3, bf16[768,2304]{1,0:T(8,128)(2,1)} %all-gather.8.cloned.1.call-done, f32[2304]{0:T(1024)S(1)} %pad_maximum_fusion.3), kind=kOutput, calls=%fused_computation.36 | convolution fusion | flops 3628597248 | bytes 9839616 | tf_op jit(solution)/shard_map/dot_general | solution.py:130
  52.1 7.2 %copy.97 = bf16[1024,2304]{0,1:T(8,128)(2,1)} copy(bf16[1024,2304]{1,0:T(8,128)(2,1)} %add_convert_fusion) | data formatting | bytes 9437184 | tf_op jit(solution)/shard_map/convert_element_type | solution.py:130
  59.3 8.9 %reshape.241 = bf16[4,256,3,12,64]{1,0,4,3,2:T(4,128)(2,1)} reshape(bf16[1024,2304]{0,1:T(8,128)(2,1)} %copy.97) | data formatting | bytes 9437184 | tf_op jit(solution)/shard_map/reshape | solution.py:133
  68.2 3.3 fusion.61
  73.4 2.7 fusion.12
  78.1 2.4 fusion.28
  83.2 3.4 fusion.63
  88.8 14.1 %all-gather.12.cloned.1.call-done = bf16[768,3072]{1,0:T(8,128)(2,1)} async-done(((bf16[192,3072]{1,0:T(8,128)(2,1)}), bf16[768,3072]{1,0:T(8,128)(2,1)}) %all-gather.12.cloned.1.call-update) | async-done | bytes 4718608 | tf_op jit(solution)/shard_map/all_gather | solution.py:117
  102.9 36.9 %fusion.2 = (bf16[1024,3072]{1,0:T(8,128)(2,1)S(1)}, f32[1024,3072]{1,0:T(8,128)}) fusion(f32[3072]{0:T(1024)S(1)} %add.230, bf16[768,3072]{1,0:T(8,128)(2,1)} %all-gather.12.cloned.1.call-done, f32[1024,768]{1,0:T(8,128)} %copy-done.11, f32[768]{0:T(1024)S(1)} %get-tuple-element.28, f32[768]{0:T(1024)S(1)} %get-tuple-element.29, ...), kind=kOutput, calls=%fused_computation.4 | convolution fusion | flops 5043388416 | bytes 26765312 | tf_op jit(solution)/shard_map/dot_general | solution.py:155
  139.7 2.7 copy-done.49
  142.5 6.9 convolution_convert_fusion
  149.4 12.3 %fusion.64 = (bf16[3072]{0:T(1024)(128)(2,1)S(1)}, bf16[1024,3072]{1,0:T(8,128)(2,1)S(1)}) fusion(f32[1024,3072]{1,0:T(8,128)} %get-tuple-element.71, f32[3072]{0:T(1024)S(1)} %add.230, bf16[1024,768]{1,0:T(8,128)(2,1)S(1)} %copy-done.18, bf16[3072,768]{1,0:T(8,128)(2,1)} %all-gather.14.cloned.1.call-done), kind=kOutput, calls=%fused_computation.160 | convolution fusion | flops 4869583872 | bytes 25184256 | tf_op jit(solution)/shard_map/dot_general | solution.py:51
  161.8 10.3 %multiply_reduce_fusion.1 = (bf16[768]{0:T(1024)(128)(2,1)S(1)}, f32[1024]{0:T(1024)S(1)}, f32[1024]{0:T(1024)S(1)}, bf16[768]{0:T(1024)(128)(2,1)S(1)}, f32[1024,768]{1,0:T(8,128)S(1)}) fusion(f32[1024,768]{1,0:T(8,128)S(1)} %copy-done.12, f32[1024]{0:T(1024)S(1)} %add_rsqrt_fusion, f32[1024]{0:T(1024)S(1)} %broadcast_multiply_fusion.4, ...), kind=kOutput, calls=%fused_computation.51 | convolution fusion | flops 4838912000 | bytes 17324032 | tf_op jit(solution)/shard_map/dot_general | solution.py:51
  175.3 2.4 convolution_convert_fusion.5
  177.8 10.5 %convolution_convert_fusion.1 = bf16[768,3072]{1,0:T(8,128)(2,1)} fusion(bf16[1024,3072]{1,0:T(8,128)(2,1)} %copy-done.48, f32[1024,768]{1,0:T(8,128)} %copy-done.11, f32[768]{0:T(1024)S(1)} %get-tuple-element.28, f32[768]{0:T(1024)S(1)} %get-tuple-element.29, f32[1024]{0:T(1024)S(1)} %add_rsqrt_fusion, f32[1024]{0:T(1024)S(1)} %broadcast_multiply_fusion.4), kind=kOutput, calls=%fused_computation.39 | convolution fusion | flops 4838129664 | bytes 14170112 | tf_op jit(solution)/shard_map/dot_general | solution.py:45
  188.8 3.6 convolution_convert_fusion.4
  194.1 2.9 reshape.244
  197.0 8.6 %bitcast_convert_fusion = (bf16[4,256,12,64]{1,3,2,0:T(8,128)(2,1)S(1)}, f32[4,12,64,256]{3,2,1,0:T(8,128)}) fusion(f32[4,12,256,256]{3,2,1,0:T(8,128)} %copy-done, f32[4,256,12]{1,2,0:T(8,128)S(1)} %log_add_fusion, bf16[4,256,12,64]{1,0,3,2:T(4,128)(2,1)S(1)} %reshape.244), kind=kOutput, calls=%fused_computation.42 | convolution fusion | flops 412876800 | bytes 18923520 | tf_op jit(solution)/shard_map/pqhk,pqhe->pkhe/dot_general | solution.py:228
  207.2 11.5 %fusion.8 = (f32[4,256,12]{1,2,0:T(8,128)S(1)}, f32[4,12,256,256]{3,2,1,0:T(8,128)}) fusion(f32[4,12,256,256]{3,2,1,0:T(8,128)} %copy-done, f32[4,256,12]{1,2,0:T(8,128)S(1)} %log_add_fusion, bf16[4,256,12,64]{1,0,3,2:T(4,128)(2,1)S(1)} %reshape.244, bf16[4,256,1,12,64]{1,0,4,3,2:T(4,128)(2,1)S(1)} %copy-done.4), kind=kOutput, calls=%fused_computation.12 | convolution fusion | flops 415223808 | bytes 28409856 | tf_op jit(solution)/shard_map/pqhe,pkhe->pqhk/dot_general | solution.py:234
  219.1 7.4 %fusion.10 = bf16[4,256,12,256]{1,3,2,0:T(8,128)(2,1)S(1)} fusion(f32[4,12,256,256]{3,2,1,0:T(8,128)} %get-tuple-element.74, f32[4,12,256,256]{3,2,1,0:T(8,128)S(1)} %bitcast.173, f32[4,256,12]{1,2,0:T(8,128)S(1)} %get-tuple-element.73, f32[4,256,12]{1,2,0:T(8,128)S(1)} %log_add_fusion), kind=kLoop, calls=%fused_computation.14 | loop fusion | flops 15728640 | bytes 31555584 | tf_op jit(solution)/shard_map/convert_element_type | solution.py:238
  226.5 2.8 bitcast_convert_fusion.1
  234.9 2.7 copy-done.22
  237.5 5.5 convolution_convert_fusion.2
  244.2 2.3 bitcast_reduce_fusion.1
  246.6 2.8 bitcast_reduce_fusion.2
  249.5 8.4 %multiply_reduce_fusion.2 = (bf16[768]{0:T(1024)(128)(2,1)S(1)}, f32[1024]{0:T(1024)S(1)}, f32[1024]{0:T(1024)S(1)}, bf16[768]{0:T(1024)(128)(2,1)S(1)}, f32[1024,768]{1,0:T(8,128)S(1)}) fusion(f32[4,256,768]{2,1,0:T(8,128)S(1)} %copy-done.2, f32[1024]{0:T(1024)S(1)} %bitcast.199, f32[1024]{0:T(1024)S(1)} %bitcast.196, f32[768]{0:T(1024)S(1)} %copy-done.30, ...), kind=kOutput, calls=%fused_computation.52 | convolution fusion | flops 3630952960 | bytes 14571520 | tf_op jit(solution)/shard_map/dot_general | solution.py:51
  258.0 3.1 select_reduce_fusion
  262.1 2.8 convert_element_type.184
  267.0 9.7 %reduce-scatter.21.cloned.1.call-done = bf16[192,3072]{1,0:T(8,128)(2,1)} async-done(((bf16[768,3072]{1,0:T(8,128)(2,1)}), bf16[192,3072]{1,0:T(8,128)(2,1)}) %reduce-scatter.21.cloned.1.call-update) | async-done | bytes 1179664 | tf_op jit(solution)/shard_map/reduce_scatter | solution.py:292
  276.7 2.9 convert_element_type.180
  281.2 38.4 %reduce-scatter.13.cloned.1.call-done = bf16[192,2304]{1,0:T(8,128)(2,1)} async-done(((bf16[768,2304]{1,0:T(8,128)(2,1)}), bf16[192,2304]{1,0:T(8,128)(2,1)}) %reduce-scatter.13.cloned.1.call-update) | async-done | bytes 884752 | tf_op jit(solution)/shard_map/reduce_scatter | solution.py:286
  319.6 2.5 convert_element_type.172
  322.3 9.4 %add_convert_fusion.1 = bf16[1024,768]{1,0:T(8,128)(2,1)} fusion(f32[1024,768]{1,0:T(8,128)S(1)} %copy-done.13, bf16[1024,3072]{1,0:T(8,128)(2,1)} %copy-done.49, bf16[3072,768]{1,0:T(8,128)(2,1)} %all-gather.14.cloned.1.call-done, f32[768]{0:T(1024)S(1)} %copy-done.42), kind=kOutput, calls=%fused_computation.63 | convolution fusion | flops 4834197504 | bytes 15731712 | tf_op jit(solution)/shard_map/dot_general | solution.py:161
  331.7 10.7 %reduce-scatter.29.cloned.1.call-done = bf16[192,14]{1,0:T(8,128)(2,1)} async-done(((bf16[768,14]{1,0:T(8,128)(2,1)}), bf16[192,14]{1,0:T(8,128)(2,1)}) %reduce-scatter.29.cloned.1.call-update) | async-done | bytes 5392
  343.3 37.7 %all-reduce = f32[14,192]{1,0:T(8,128)S(1)} all-reduce(bf16[14,192]{1,0:T(8,128)(2,1)S(1)} %copy.118), channel_id=11, replica_groups=mesh['batch'=8,'fsdp'=4] {'batch'}, use_global_device_ids=true, to_apply=%region_32.33.clone | all-reduce | flops 2688 | bytes 16128
  381.7 30.8 %all-gather.1 = bf16[8,24,14]{1,2,0:T(8,128)(2,1)S(1)} all-gather(bf16[1,24,14]{1,2,0:T(8,128)(2,1)S(1)} %get-tuple-element.37), channel_id=1, replica_groups=mesh['batch'=8,'fsdp'=4] {'batch'}, dimensions={0}, use_global_device_ids=true | all-gather | bytes 6048 | tf_op jit(solution)/shard_map/all_gather | solution.py:336
  413.3 3.4 reduce-scatter.27.cloned.1.call-done
  419.5 63.1 %reduce-scatter.19.cloned.1.call-done = f32[24,768]{1,0:T(8,128)} async-done(((f32[192,768]{1,0:T(8,128)}), f32[24,768]{1,0:T(8,128)}) %reduce-scatter.19.cloned.1.call-update) | async-done | bytes 73744 | tf_op jit(solution)/shard_map/reduce_scatter | solution.py:304
  484.2 31.7 %all_gather.38 = bf16[192,768]{1,0:T(8,128)(2,1)S(1)} all-gather(bf16[24,768]{1,0:T(8,128)(2,1)S(1)} %get-tuple-element.49), channel_id=1, replica_groups=mesh['batch'=8,'fsdp'=4] {'batch'}, dimensions={0}, use_global_device_ids=true | all-gather | bytes 331776 | tf_op jit(solution)/shard_map/all_gather | solution.py:329
  516.9 40.5 %reduce-scatter.23.cloned.1.call-done = f32[24,3072]{1,0:T(8,128)} async-done(((f32[192,3072]{1,0:T(8,128)}), f32[24,3072]{1,0:T(8,128)}) %reduce-scatter.23.cloned.1.call-update) | async-done | bytes 294928 | tf_op jit(solution)/shard_map/reduce_scatter | solution.py:305
  561.1 73.6 %reduce-scatter.15.cloned.1.call-done = f32[24,2304]{1,0:T(8,128)} async-done(((f32[192,2304]{1,0:T(8,128)}), f32[24,2304]{1,0:T(8,128)}) %reduce-scatter.15.cloned.1.call-update) | async-done | bytes 221200 | tf_op jit(solution)/shard_map/reduce_scatter | solution.py:303
  636.7 34.1 %all_gather.37 = bf16[192,2304]{1,0:T(8,128)(2,1)S(1)} all-gather(bf16[24,2304]{1,0:T(8,128)(2,1)S(1)} %get-tuple-element.52), channel_id=1, replica_groups=mesh['batch'=8,'fsdp'=4] {'batch'}, dimensions={0}, use_global_device_ids=true | all-gather | bytes 995328 | tf_op jit(solution)/shard_map/all_gather | solution.py:326
  674.2 6.6 all-gather.16.cloned.1.call-done
  680.8 2.9 convert_element_type.182
  (224 shorter events, 53.4 us)
Async XLA Ops:
  7.2 36.4 %all-gather.8.cloned.1.call-start = ((), (), s32[]{:S(2)}) async-start(), calls=%async_computation.9 | async-start | bytes 4423680 | tf_op jit(solution)/shard_map/all_gather | solution.py:115
  9.9 73.3 %all-gather.10.cloned.1.call-start = ((), (), s32[]{:S(2)}) async-start(), calls=%async_computation.10 | async-start | bytes 1474560 | tf_op jit(solution)/shard_map/all_gather | solution.py:116
  10.7 92.1 %all-gather.12.cloned.1.call-start = ((), (), s32[]{:S(2)}) async-start(), calls=%async_computation.11 | async-start | bytes 5898240 | tf_op jit(solution)/shard_map/all_gather | solution.py:117
  12.0 10.1 %copy-start.46 = (s32[4]{0:T(128)S(1)}, s32[4]{0:T(128)}, u32[]{:S(2)}) copy-start(s32[4]{0:T(128)} %param.22) | copy-start | bytes 52
  12.0 10.2 %copy-start.43 = (s32[4,128]{1,0:T(4,128)S(1)}, s32[4,128]{1,0:T(4,128)}, u32[]{:S(2)}) copy-start(s32[4,128]{1,0:T(4,128)} %param.21) | copy-start | bytes 6148
  12.0 11.1 %copy-start.16 = (bf16[4,256,768]{2,1,0:T(8,128)(2,1)S(1)}, bf16[4,256,768]{2,1,0:T(8,128)(2,1)}, u32[]{:S(2)}) copy-start(bf16[4,256,768]{2,1,0:T(8,128)(2,1)} %param.19) | copy-start | bytes 4718596
  12.0 137.4 %all-gather.14.cloned.1.call-start = ((), (), s32[]{:S(2)}) async-start(), calls=%async_computation.12 | async-start | bytes 5898240 | tf_op jit(solution)/shard_map/all_gather | solution.py:118
  15.0 247.1 %reduce-scatter.25.cloned.1.call-start = ((), (), s32[]{:S(2)}) async-start(), calls=%async_computation.20 | async-start | bytes 5898240 | tf_op jit(solution)/shard_map/reduce_scatter | solution.py:295
  15.1 8.0 %copy-start.44 = (pred[256]{0:T(512)(128)(4,1)}, pred[256]{0:T(512)(128)(4,1)S(1)}, u32[]{:S(2)}) copy-start(pred[256]{0:T(512)(128)(4,1)S(1)} %iota_compare_fusion.2) | copy-start | bytes 772
  22.1 5.6 copy-start.29
  25.8 57.4 %copy-start.1 = (f32[4,256,768]{2,1,0:T(8,128)}, f32[4,256,768]{2,1,0:T(8,128)S(1)}, u32[]{:S(2)}) copy-start(f32[4,256,768]{2,1,0:T(8,128)S(1)} %get-tuple-element.59) | copy-start | bytes 9437188
  102.9 39.6 %copy-start.18 = (bf16[1024,768]{1,0:T(8,128)(2,1)S(1)}, bf16[1024,768]{1,0:T(8,128)(2,1)}, u32[]{:S(2)}) copy-start(bf16[1024,768]{1,0:T(8,128)(2,1)} %fusion.27) | copy-start | bytes 4718596
  149.4 115.7 %reduce-scatter.17.cloned.1.call-start = ((), (), s32[]{:S(2)}) async-start(), calls=%async_computation.15 | async-start | bytes 1474560 | tf_op jit(solution)/shard_map/reduce_scatter | solution.py:289
  149.4 12.4 %copy-start.12 = (f32[1024,768]{1,0:T(8,128)S(1)}, f32[1024,768]{1,0:T(8,128)}, u32[]{:S(2)}) copy-start(f32[1024,768]{1,0:T(8,128)} %copy-done.11) | copy-start | bytes 9437188
  161.8 10.4 %copy-start.48 = (bf16[1024,3072]{1,0:T(8,128)(2,1)}, bf16[1024,3072]{1,0:T(8,128)(2,1)S(1)}, u32[]{:S(2)}) copy-start(bf16[1024,3072]{1,0:T(8,128)(2,1)S(1)} %get-tuple-element.81) | copy-start | bytes 18874372
  161.8 10.4 %copy-start.8 = (bf16[4,256,768]{2,1,0:T(8,128)(2,1)S(1)}, bf16[4,256,768]{2,1,0:T(8,128)(2,1)}, u32[]{:S(2)}) copy-start(bf16[4,256,768]{2,1,0:T(8,128)(2,1)} %param.20) | copy-start | bytes 4718596
  161.8 10.4 %copy-start.36 = (f32[1,2,4,128]{3,1,2,0:T(2,128)S(1)}, f32[1,2,4,128]{3,1,2,0:T(2,128)}, u32[]{:S(2)}) copy-start(f32[1,2,4,128]{3,1,2,0:T(2,128)} %copy-done.35) | copy-start | bytes 12292
  177.7 98.9 %reduce-scatter.21.cloned.1.call-start = ((), (), s32[]{:S(2)}) async-start(), calls=%async_computation.17 | async-start | bytes 5898240 | tf_op jit(solution)/shard_map/reduce_scatter | solution.py:292
  188.3 131.3 %reduce-scatter.13.cloned.1.call-start = ((), (), s32[]{:S(2)}) async-start(), calls=%async_computation.13 | async-start | bytes 4423680 | tf_op jit(solution)/shard_map/reduce_scatter | solution.py:286
  206.8 11.9 %slice-start = ((s8[12582912]{0:T(1024)(128)(4,1)}), s8[4194304]{0:T(1024)(128)(4,1)S(1)}, s32[]{:S(2)}) async-start(s8[12582912]{0:T(1024)(128)(4,1)} %bitcast.172), calls=%async_computation.23 | async-start | bytes 8388608
  207.2 11.5 %slice-start.1 = ((s8[12582912]{0:T(1024)(128)(4,1)}), s8[4194304]{0:T(1024)(128)(4,1)S(1)}, s32[]{:S(2)}) async-start(s8[12582912]{0:T(1024)(128)(4,1)} %bitcast.172), calls=%async_computation.24 | async-start | bytes 8388608
  207.2 11.9 %slice-start.2 = ((s8[12582912]{0:T(1024)(128)(4,1)}), s8[4194304]{0:T(1024)(128)(4,1)S(1)}, s32[]{:S(2)}) async-start(s8[12582912]{0:T(1024)(128)(4,1)} %bitcast.172), calls=%async_computation.25 | async-start | bytes 8388608
  219.1 7.4 %copy-start.10 = (bf16[4,256,1,12,64]{1,0,4,3,2:T(4,128)(2,1)S(1)}, bf16[4,256,1,12,64]{1,0,4,3,2:T(4,128)(2,1)}, u32[]{:S(2)}) copy-start(bf16[4,256,1,12,64]{1,0,4,3,2:T(4,128)(2,1)} %copy-done.9) | copy-start | bytes 4718596
  243.1 99.4 %reduce-scatter.29.cloned.1.call-start = ((), (), s32[]{:S(2)}) async-start(), calls=%async_computation.22 | async-start | bytes 245760
  244.2 5.3 copy-start.2
  244.2 5.3 copy-start.30
  244.2 5.3 copy-start.32
  249.5 8.5 %copy-start.15 = (f32[1024,768]{1,0:T(8,128)S(1)}, f32[1024,768]{1,0:T(8,128)}, u32[]{:S(2)}) copy-start(f32[1024,768]{1,0:T(8,128)} %copy-done.14) | copy-start | bytes 9437188
  262.1 154.6 %reduce-scatter.27.cloned.1.call-start = ((), (), s32[]{:S(2)}) async-start(), calls=%async_computation.21 | async-start | bytes 2654208 | tf_op jit(solution)/shard_map/reduce_scatter | solution.py:306
  265.0 217.6 %reduce-scatter.19.cloned.1.call-start = ((), (), s32[]{:S(2)}) async-start(), calls=%async_computation.16 | async-start | bytes 663552 | tf_op jit(solution)/shard_map/reduce_scatter | solution.py:304
  266.9 12.8 %copy-start.47 = (u32[32]{0:T(128)S(1)}, u32[32]{0:T(128)}, u32[]{:S(2)}) copy-start(u32[32]{0:T(128)} %constant.163) | copy-start | bytes 388
  266.9 290.5 %reduce-scatter.23.cloned.1.call-start = ((), (), s32[]{:S(2)}) async-start(), calls=%async_computation.18 | async-start | bytes 2654208 | tf_op jit(solution)/shard_map/reduce_scatter | solution.py:305
  279.6 42.6 %copy-start.13 = (f32[1024,768]{1,0:T(8,128)S(1)}, f32[1024,768]{1,0:T(8,128)}, u32[]{:S(2)}) copy-start(f32[1024,768]{1,0:T(8,128)} %copy-done.11) | copy-start | bytes 9437188
  279.6 42.6 %copy-start.42 = (f32[768]{0:T(1024)S(1)}, f32[768]{0:T(1024)}, u32[]{:S(2)}) copy-start(f32[768]{0:T(1024)} %get-tuple-element.27) | copy-start | bytes 9220
  279.6 355.1 %reduce-scatter.15.cloned.1.call-start = ((), (), s32[]{:S(2)}) async-start(), calls=%async_computation.14 | async-start | bytes 1990656 | tf_op jit(solution)/shard_map/reduce_scatter | solution.py:303
  322.2 358.6 %all-gather.16.cloned.1.call-start = ((), (), s32[]{:S(2)}) async-start(), calls=%async_computation.19 | async-start | bytes 1327104 | tf_op jit(solution)/shard_map/all_gather | solution.py:332
  322.2 58.8 %copy-start.38 = (f32[14,192]{1,0:T(8,128)S(1)}, f32[14,192]{1,0:T(8,128)}, u32[]{:S(2)}) copy-start(f32[14,192]{1,0:T(8,128)} %param.35) | copy-start | bytes 32260
  322.2 58.8 %copy-start.40 = (f32[14,24]{1,0:T(8,128)S(1)}, f32[14,24]{1,0:T(8,128)}, u32[]{:S(2)}) copy-start(f32[14,24]{1,0:T(8,128)} %param.36) | copy-start | bytes 4036
  322.3 58.8 %copy-start.41 = (f32[14,24]{1,0:T(8,128)S(1)}, f32[14,24]{1,0:T(8,128)}, u32[]{:S(2)}) copy-start(f32[14,24]{1,0:T(8,128)} %param.37) | copy-start | bytes 4036
  322.3 94.4 %copy-start.23 = (f32[96,768]{1,0:T(8,128)S(1)}, f32[96,768]{1,0:T(8,128)}, u32[]{:S(2)}) copy-start(f32[96,768]{1,0:T(8,128)} %param.33) | copy-start | bytes 884740
  322.3 160.3 %copy-start.28 = (f32[24,768]{1,0:T(8,128)S(1)}, f32[24,768]{1,0:T(8,128)}, u32[]{:S(2)}) copy-start(f32[24,768]{1,0:T(8,128)} %param.27) | copy-start | bytes 221188
  331.7 225.7 %copy-start.24 = (f32[24,3072]{1,0:T(8,128)S(1)}, f32[24,3072]{1,0:T(8,128)}, u32[]{:S(2)}) copy-start(f32[24,3072]{1,0:T(8,128)} %param.30) | copy-start | bytes 884740
  331.7 225.7 %copy-start.25 = (f32[24,3072]{1,0:T(8,128)S(1)}, f32[24,3072]{1,0:T(8,128)}, u32[]{:S(2)}) copy-start(f32[24,3072]{1,0:T(8,128)} %param.31) | copy-start | bytes 884740
  418.8 97.9 %collective-permute-start = (bf16[1,96,768]{2,1,0:T(8,128)(2,1)S(1)}, bf16[1,96,768]{2,1,0:T(8,128)(2,1)S(1)}, u32[]{:S(2)}, u32[]{:S(2)}) collective-permute-start(bf16[1,96,768]{2,1,0:T(8,128)(2,1)S(1)} %bitcast.187), channel_id=1, source_target_pairs={{0,4},{4,0},{8,12},{12,8},{16,20},{20,16},{24,28},{28,24},{1,5},{5... | collective-permute-start | bytes 442376 | tf_op jit(solution)/shard_map/ppermute | solution.py:37
  516.7 118.0 %copy-start.26 = (f32[24,2304]{1,0:T(8,128)S(1)}, f32[24,2304]{1,0:T(8,128)}, u32[]{:S(2)}) copy-start(f32[24,2304]{1,0:T(8,128)} %param.24) | copy-start | bytes 663556
  516.7 118.0 %copy-start.27 = (f32[24,2304]{1,0:T(8,128)S(1)}, f32[24,2304]{1,0:T(8,128)}, u32[]{:S(2)}) copy-start(f32[24,2304]{1,0:T(8,128)} %param.25) | copy-start | bytes 663556
  516.8 42.6 %collective-permute-start.1 = (bf16[2,96,768]{2,1,0:T(8,128)(2,1)S(1)}, bf16[2,96,768]{2,1,0:T(8,128)(2,1)S(1)}, u32[]{:S(2)}, u32[]{:S(2)}) collective-permute-start(bf16[2,96,768]{2,1,0:T(8,128)(2,1)S(1)} %get-tuple-element.61), channel_id=1, source_target_pairs={{0,8},{4,12},{8,0},{12,4},{16,24},{20,28},{24,16},{28,20},{1,9},{5... | collective-permute-start | bytes 884744 | tf_op jit(solution)/shard_map/ppermute | solution.py:37
  559.7 112.5 %collective-permute-start.2 = (bf16[4,96,768]{2,1,0:T(8,128)(2,1)S(1)}, bf16[4,96,768]{2,1,0:T(8,128)(2,1)S(1)}, u32[]{:S(2)}, u32[]{:S(2)}) collective-permute-start(bf16[4,96,768]{2,1,0:T(8,128)(2,1)S(1)} %bitcast.182), channel_id=1, source_target_pairs={{0,16},{4,20},{8,24},{12,28},{16,0},{20,4},{24,8},{28,12},{1,17},{... | collective-permute-start | bytes 1769480 | tf_op jit(solution)/shard_map/ppermute | solution.py:37
  (22 other events, 58.4 us)
Sparse Core Ops, SparseCore 0:
  10.2 33.4 all-gather.7
  45.8 17.4 all-gather.9
  65.4 37.4 all-gather.11
  104.3 37.4 all-gather.13
  149.5 47.9 reduce-scatter.24
  200.5 25.6 reduce-scatter.16
  228.7 47.9 reduce-scatter.20
  279.2 40.3 reduce-scatter.12
  322.7 19.7 reduce-scatter.28
  346.4 70.2 reduce-scatter.26
  420.6 61.9 reduce-scatter.18
  486.5 70.8 reduce-scatter.22
  561.4 73.2 reduce-scatter.14
  637.4 43.3 all-gather.15
